TPU v7x, 32 devices: a whole 2x2x4 slice. The times are simulated.
32 devices in a mesh: grp: 2 (over core), dp: 16 (over z, y, x).
Axes of the slice: x: 2, y: 2, z: 4, core: 2. Of those that a mesh axis runs over, the one named last changes fastest.
Arguments:
- hidden: bfloat16 [32768, 768], P(('grp', 'dp')), may hold values from -6 to 6
- grad_out: bfloat16 [32768, 768], P(('grp', 'dp')), may hold values from -6 to 6
- seq_lens: int32 [64], P(('grp', 'dp')), may hold values from 128 to 512, as said below
- mix_state: float32 [4, 5, 768, 384], P(None, None, ('grp', 'dp')), as said below
- out_state: float32 [4, 768, 768], P(None, ('grp', 'dp')), as said below
- depth_state: float32 [4, 9, 768], replicated, as said below
- span_state: float32 [4, 384, 54], replicated, as said below
- norm_state: float32 [4, 4, 768], replicated, as said below
- up_state: float32 [4, 2, 384, 1536], P(None, 'grp', None, 'dp'), as said below
- bias_state: float32 [4, 2, 1536], P(None, 'grp', 'dp'), as said below
- down_state: float32 [4, 2, 1536, 384], P(None, 'grp', 'dp'), as said below
Outputs:
- out: bfloat16 [32768, 768], P(('grp', 'dp'))
- input_grad: bfloat16 [32768, 768], P(('grp', 'dp'))
- mix_new: float32 [2, 5, 768, 384], P(None, None, ('grp', 'dp'))
- mix_moments: float32 [2, 5, 768, 384], P(None, None, ('grp', 'dp'))
- out_new: float32 [2, 768, 768], P(None, ('grp', 'dp'))
- out_moments: float32 [2, 768, 768], P(None, ('grp', 'dp'))
- depth_new: float32 [2, 9, 768], replicated
- depth_moments: float32 [2, 9, 768], replicated
- span_new: float32 [2, 384, 54], replicated
- span_moments: float32 [2, 384, 54], replicated
- norm_new: float32 [2, 4, 768], replicated
- norm_moments: float32 [2, 4, 768], replicated
- up_new: float32 [2, 2, 384, 1536], P(None, 'grp', None, 'dp')
- up_moments: float32 [2, 2, 384, 1536], P(None, 'grp', None, 'dp')
- bias_new: float32 [2, 2, 1536], P(None, 'grp', 'dp')
- bias_moments: float32 [2, 2, 1536], P(None, 'grp', 'dp')
- down_new: float32 [2, 2, 1536, 384], P(None, 'grp', 'dp')
- down_moments: float32 [2, 2, 1536, 384], P(None, 'grp', 'dp')
Inputs may be any that keep to these rules, and one draw needn't show every extreme that they name: The first seq_lens positions of a sequence are live keys, the rest padding; the first sequence is full. `mix_state`: slot 2 is positive. `out_state`: slot 2 is positive. `depth_state`: slot 2 is positive. `span_state`: slot 2 is positive. `norm_state`: slot 2 is positive. `up_state`: slot 2 is positive. `bias_state`: slot 2 is positive. `down_state`: slot 2 is positive.
All inputs are finite; a program needn't handle non-finite values.
Results may differ from a plain program's by a relative error of at most 0.029.
Values may be sent and summed in bfloat16 or wider, within the bound.
No kernel may reach another device: no remote copies, remote signals or barrier semaphores. Data moves between devices by JAX's collectives and lax.ppermute only.
A program may use at most 192 MiB of HBM per device.

v0:
```python
import jax
import jax.numpy as jnp
from jax import lax
from jax.sharding import PartitionSpec as P

HEADS = 6
HS = 64
KERNEL = 9
STEP = 7
beta_one = 0.9
beta_two = 0.999
adam_eps = 1e-06
ema_rate = 0.99
decay_rate = 0.01
rate_mix = 0.06
rate_out = 0.12
rate_depth = 0.4
rate_span = 0.08
rate_norm = 0.5
rate_up = 0.08
rate_bias = 0.3
rate_down = 0.04


def rounded(value):
    return value.astype(jnp.bfloat16).astype(jnp.float32)


def softmax_rows(scores):
    top_score = jnp.max(scores, axis=-1, keepdims=True)
    powers = jnp.exp(scores - top_score)
    return powers / jnp.sum(powers, axis=-1, keepdims=True)


def gelu_exact(value):
    return 0.5 * value * (1.0 + lax.erf(value * 2.0 ** (-0.5)))


def layer_norm(value, scale_row, shift_row):
    centered = value - jnp.mean(value, axis=-1, keepdims=True)
    variance = jnp.mean(centered * centered, axis=-1, keepdims=True)
    return centered * lax.rsqrt(variance + 1e-12) * scale_row + shift_row


def rear_norm(summed, norms):
    return layer_norm(summed, norms[2], norms[3])


def front_part(inputs, mix, depth, span):
    count, length, width = inputs.shape
    reach = KERNEL // 2
    flat = inputs.reshape(count * length, width)
    queries = rounded(jnp.dot(flat, mix[0]))
    key_rows = rounded(jnp.dot(flat, mix[1]))
    value_rows = rounded(jnp.dot(flat, mix[2]))
    padded = jnp.pad(inputs, ((0, 0), (reach, reach), (0, 0)))
    spread = depth[0] * padded[:, 0:length]
    for offset in range(1, KERNEL):
        spread = spread + depth[offset] * padded[:, offset : offset + length]
    conv_in = rounded(spread.reshape(count * length, width))
    conv_keys = rounded(jnp.dot(conv_in, mix[3]))
    joined = rounded(conv_keys * queries)
    logits = rounded(jnp.dot(joined, span)).reshape(count, length, HEADS, KERNEL)
    kernel_w = softmax_rows(logits)
    conv_vals = rounded(jnp.dot(flat, mix[4])).reshape(count, length, HEADS, HS)
    conv_pad = jnp.pad(conv_vals, ((0, 0), (reach, reach), (0, 0), (0, 0)))
    convolved = kernel_w[..., 0:1] * conv_pad[:, 0:length]
    for offset in range(1, KERNEL):
        convolved = (
            convolved + kernel_w[..., offset : offset + 1] * conv_pad[:, offset : offset + length]
        )
    return (queries, key_rows, value_rows, convolved.reshape(count * length, width // 2))


def back_part(context, convolved, flat, w_out, norms):
    mixed = rounded(jnp.concatenate([context, convolved], axis=1))
    branch = rounded(jnp.dot(mixed, w_out))
    return layer_norm(branch + flat, norms[0], norms[1])


def scores_of(queries, key_rows, seq_len):
    scores = jnp.einsum(
        "qhd,khd->hqk",
        queries.astype(jnp.bfloat16),
        key_rows.astype(jnp.bfloat16),
        preferred_element_type=jnp.float32,
    ) * HS ** (-0.5)
    places = lax.broadcasted_iota(jnp.int32, scores.shape, 2)
    return jnp.where(places < seq_len, scores, -1000000000.0)


def attend_forward(queries, key_rows, value_rows, seq_len):
    scores = scores_of(queries, key_rows, seq_len)
    top_score = jnp.max(scores, axis=-1, keepdims=True)
    powers = jnp.exp(scores - top_score)
    total = jnp.sum(powers, axis=-1, keepdims=True)
    weights = (powers / total).astype(jnp.bfloat16)
    context = jnp.einsum(
        "hqk,khd->qhd", weights, value_rows.astype(jnp.bfloat16), preferred_element_type=jnp.float32
    )
    return (context, top_score + jnp.log(total))


def attend_backward(queries, key_rows, value_rows, seq_len, log_total, d_context):
    query_low = queries.astype(jnp.bfloat16)
    key_low = key_rows.astype(jnp.bfloat16)
    scores = scores_of(queries, key_rows, seq_len)
    probs = jnp.exp(scores - log_total)
    weights = probs.astype(jnp.bfloat16)
    context_low = d_context.astype(jnp.bfloat16)
    d_weights = rounded(
        jnp.einsum(
            "qhd,khd->hqk",
            context_low,
            value_rows.astype(jnp.bfloat16),
            preferred_element_type=jnp.float32,
        )
    )
    d_scores = (probs * (d_weights - jnp.sum(probs * d_weights, axis=-1, keepdims=True))).astype(
        jnp.bfloat16
    )
    d_queries = jnp.einsum(
        "hqk,khd->qhd", d_scores, key_low, preferred_element_type=jnp.float32
    ) * HS ** (-0.5)
    d_keys = jnp.einsum(
        "hqk,qhd->khd", d_scores, query_low, preferred_element_type=jnp.float32
    ) * HS ** (-0.5)
    d_values = jnp.einsum("hqk,qhd->khd", weights, context_low, preferred_element_type=jnp.float32)
    return (d_queries, d_keys, d_values)


def adamw(opt_state, gradient, step_rate, wd_rate):
    moment_one = beta_one * opt_state[1] + (1.0 - beta_one) * gradient
    moment_two = beta_two * opt_state[2] + (1.0 - beta_two) * gradient * gradient
    scaled_one = moment_one / (1.0 - beta_one**STEP)
    scaled_two = moment_two / (1.0 - beta_two**STEP)
    weight = opt_state[0] - step_rate * (
        scaled_one / (jnp.sqrt(scaled_two) + adam_eps) + wd_rate * opt_state[0]
    )
    average = ema_rate * opt_state[3] + (1.0 - ema_rate) * weight
    return (jnp.stack([weight, average]), jnp.stack([moment_one, moment_two]))


def on_device(
    hidden,
    grad_out,
    seq_lens,
    mix_state,
    out_state,
    depth_state,
    span_state,
    norm_state,
    up_state,
    bias_state,
    down_state,
):
    tokens_dev, width = hidden.shape
    count = seq_lens.shape[0]
    length = tokens_dev // count
    half = width // 2
    shaped = (count, length, HEADS, HS)
    inputs = hidden.astype(jnp.float32).reshape(count, length, width)
    flat = inputs.reshape(tokens_dev, width)
    depth_w = rounded(depth_state[0])
    span_w = rounded(span_state[0])
    norm_w = norm_state[0]
    mix_low = mix_state[0].astype(jnp.bfloat16)
    out_low = out_state[0].astype(jnp.bfloat16)

    def mixer_pass(mix_all, out_all):
        front_out, front_back = jax.vjp(
            front_part, inputs, mix_all.astype(jnp.float32), depth_w, span_w
        )
        queries, key_rows, value_rows, convolved = front_out
        context, log_total = jax.vmap(attend_forward)(
            queries.reshape(shaped), key_rows.reshape(shaped), value_rows.reshape(shaped), seq_lens
        )
        normed, rear_back = jax.vjp(
            back_part,
            context.reshape(tokens_dev, half),
            convolved,
            flat,
            out_all.astype(jnp.float32),
            norm_w,
        )
        return (normed, (front_back, rear_back, queries, key_rows, value_rows, log_total))

    mix_all, out_all = (
        lax.all_gather(mix_low, ("grp", "dp"), axis=1, tiled=True),
        lax.all_gather(out_low, ("grp", "dp"), axis=0, tiled=True),
    )
    normed, saved = mixer_pass(mix_all, out_all)
    up_all, bias_all, down_all = (
        lax.all_gather(up_state[0, 0].astype(jnp.bfloat16), "dp", axis=1, tiled=True),
        lax.all_gather(bias_state[0, 0].astype(jnp.bfloat16), "dp", axis=0, tiled=True),
        lax.all_gather(down_state[0, 0].astype(jnp.bfloat16), "dp", axis=0, tiled=True),
    )
    group_in = lax.all_to_all(
        normed.astype(jnp.bfloat16), "grp", split_axis=1, concat_axis=0, tiled=True
    )
    pre_act = jnp.dot(group_in, up_all, preferred_element_type=jnp.float32) + bias_all.astype(
        jnp.float32
    )
    act_low = gelu_exact(pre_act).astype(jnp.bfloat16)
    group_out = jnp.dot(act_low, down_all, preferred_element_type=jnp.float32).astype(jnp.bfloat16)
    back_out = lax.all_to_all(group_out, "grp", split_axis=0, concat_axis=1, tiled=True)
    summed = normed + back_out.astype(jnp.float32)
    result, norm_back = jax.vjp(rear_norm, summed, norm_w)
    d_summed, d_norms_two = norm_back(grad_out.astype(jnp.float32))
    d_group_out = lax.all_to_all(
        d_summed.astype(jnp.bfloat16), "grp", split_axis=1, concat_axis=0, tiled=True
    )
    d_act = lax.dot_general(
        d_group_out, down_all, (((1,), (1,)), ((), ())), preferred_element_type=jnp.float32
    )
    gelu_value, gelu_back = jax.vjp(gelu_exact, pre_act)
    d_pre = gelu_back(d_act)[0].astype(jnp.bfloat16)
    d_down = lax.dot_general(
        act_low, d_group_out, (((0,), (0,)), ((), ())), preferred_element_type=jnp.float32
    )
    d_up = lax.dot_general(
        group_in, d_pre, (((0,), (0,)), ((), ())), preferred_element_type=jnp.float32
    )
    d_bias = jnp.sum(d_pre, axis=0, dtype=jnp.float32)
    d_group_in = lax.dot_general(
        d_pre, up_all, (((1,), (1,)), ((), ())), preferred_element_type=jnp.float32
    ).astype(jnp.bfloat16)
    d_back_in = lax.all_to_all(d_group_in, "grp", split_axis=0, concat_axis=1, tiled=True)
    d_normed = d_summed + d_back_in.astype(jnp.float32)
    mix_again, out_again = (
        lax.all_gather(mix_low, ("grp", "dp"), axis=1, tiled=True),
        lax.all_gather(out_low, ("grp", "dp"), axis=0, tiled=True),
    )
    mixer_saved = mixer_pass(mix_again, out_again)[1]
    front_back, rear_back, queries, key_rows, value_rows, log_total = mixer_saved
    d_context, d_convolved, d_flat, d_out, d_norms = rear_back(d_normed)
    d_queries, d_keys, d_values = jax.vmap(attend_backward)(
        queries.reshape(shaped),
        key_rows.reshape(shaped),
        value_rows.reshape(shaped),
        seq_lens,
        log_total,
        d_context.reshape(shaped),
    )
    d_inputs, d_mix, d_depth, d_span = front_back(
        (
            d_queries.reshape(tokens_dev, half),
            d_keys.reshape(tokens_dev, half),
            d_values.reshape(tokens_dev, half),
            d_convolved,
        )
    )
    d_inputs, d_mix, d_out, d_depth, d_span, d_norms_one = (
        d_inputs.reshape(tokens_dev, width) + d_flat,
        d_mix,
        d_out,
        d_depth,
        d_span,
        d_norms,
    )
    mix_grad, out_grad = (
        lax.psum_scatter(d_mix, ("grp", "dp"), scatter_dimension=1, tiled=True),
        lax.psum_scatter(d_out, ("grp", "dp"), scatter_dimension=0, tiled=True),
    )
    up_grad, bias_grad, down_grad = (
        lax.psum_scatter(d_up, "dp", scatter_dimension=1, tiled=True),
        lax.psum_scatter(d_bias, "dp", scatter_dimension=0, tiled=True),
        lax.psum_scatter(d_down, "dp", scatter_dimension=0, tiled=True),
    )
    depth_grad, span_grad, norm_grad = lax.psum(
        (d_depth, d_span, d_norms_one + d_norms_two), ("grp", "dp")
    )
    mix_update = adamw(mix_state, mix_grad, rate_mix, decay_rate)
    out_update = adamw(out_state, out_grad, rate_out, decay_rate)
    depth_update = adamw(depth_state, depth_grad, rate_depth, decay_rate)
    span_update = adamw(span_state, span_grad, rate_span, decay_rate)
    norm_update = adamw(norm_state, norm_grad, rate_norm, 0.0)
    up_update = adamw(up_state, up_grad[None], rate_up, decay_rate)
    bias_update = adamw(bias_state, bias_grad[None], rate_bias, 0.0)
    down_update = adamw(down_state, down_grad[None], rate_down, decay_rate)
    return (
        result.astype(jnp.bfloat16),
        d_inputs.astype(jnp.bfloat16),
        mix_update[0],
        mix_update[1],
        out_update[0],
        out_update[1],
        depth_update[0],
        depth_update[1],
        span_update[0],
        span_update[1],
        norm_update[0],
        norm_update[1],
        up_update[0],
        up_update[1],
        bias_update[0],
        bias_update[1],
        down_update[0],
        down_update[1],
    )


def solution(mesh):
    placed = (
        P(("grp", "dp"), None),
        P(("grp", "dp"), None),
        P(("grp", "dp")),
        P(None, None, ("grp", "dp"), None),
        P(None, ("grp", "dp"), None),
        P(),
        P(),
        P(),
        P(None, "grp", None, "dp"),
        P(None, "grp", "dp"),
        P(None, "grp", "dp", None),
    )
    return jax.shard_map(
        on_device,
        mesh=mesh,
        in_specs=placed,
        out_specs=(
            P(("grp", "dp"), None),
            P(("grp", "dp"), None),
            P(None, None, ("grp", "dp"), None),
            P(None, None, ("grp", "dp"), None),
            P(None, ("grp", "dp"), None),
            P(None, ("grp", "dp"), None),
            P(),
            P(),
            P(),
            P(),
            P(),
            P(),
            P(None, "grp", None, "dp"),
            P(None, "grp", None, "dp"),
            P(None, "grp", "dp"),
            P(None, "grp", "dp"),
            P(None, "grp", "dp", None),
            P(None, "grp", "dp", None),
        ),
        check_vma=False,
    )
```

profile of v0, /device:TPU:0, one launch (start us, length us, event | category | flops | bytes accessed | tf_op | source)
XLA Modules:
  0.0 987.0 jit_solution(7047482871832338159)
XLA Ops:
  16.7 43.7 %all-reduce.47 = bf16[1536]{0:T(1024)(128)(2,1)S(1)} all-reduce(bf16[1536]{0:T(1024)(128)(2,1)S(1)} %dynamic-update-slice), channel_id=1, replica_groups=mesh['grp'=2,'dp'=16] {'dp'}, use_global_device_ids=true, to_apply=%add.47 | all-reduce | flops 1536 | bytes 6144
  71.0 4.1 reshape.438
  75.1 39.1 %add_convert_fusion.3 = bf16[2,512,768]{1,0,2:T(2,128)(2,1)S(1)} fusion(f32[2,512,768]{1,0,2:T(2,128)} %reshape.438, f32[768]{0:T(1024)S(1)} %get-tuple-element.102, f32[768]{0:T(1024)S(1)} %get-tuple-element.103, f32[768]{0:T(1024)S(1)} %get-tuple-element.104, f32[768]{0:T(1024)S(1)} %get-tuple-element.105, f32[768]{0:T(1024)S(1)} %get-tuple-element.106, ...), kind=kLoop, calls=%fused_computation.58 | loop fusion | flops 14155776 | bytes 4746240 | tf_op jit(solution)/shard_map/jvp()/convert_element_type | solution.py:26
  120.2 3.4 convolution_convert_fusion.8
  132.7 3.9 fusion.22
  136.7 3.0 copy.141
  139.7 3.6 reshape.464
  147.8 18.1 %add_convert_fusion.6 = bf16[2,512,6,64]{1,0,3,2:T(2,128)(2,1)S(1)} fusion(f32[2,512,6,64]{1,0,3,2:T(2,128)} %reshape.464, f32[2,512,6]{1,0,2:T(2,128)S(1)} %get-tuple-element.181, f32[2,512,6]{1,0,2:T(2,128)S(1)} %get-tuple-element.182, f32[2,512,6]{1,0,2:T(2,128)S(1)} %get-tuple-element.183, f32[2,512,6]{1,0,2:T(2,128)S(1)} %get-tuple-element.184, ...), kind=kLoop, calls=%fused_computation.103 | loop fusion | flops 7077888 | bytes 2580480 | tf_op jit(solution)/shard_map/convert.9
  166.1 3.0 fusion.130
  173.8 2.7 fusion.31
  179.4 3.3 fusion.21
  188.5 4.6 all-to-all-start
  195.8 10.4 %multiply_convert_fusion = (bf16[2048,1536]{1,0:T(8,128)(2,1)}, f32[2048,1536]{1,0:T(8,128)}) fusion(f32[1536]{0:T(1024)} %convert_element_type.299, bf16[2048,384]{1,0:T(8,128)(2,1)} %bitcast.21, bf16[384,1536]{0,1:T(8,128)(2,1)} %all-gather.9.cloned.1.call-done), kind=kOutput, calls=%fused_computation.8 | convolution fusion | flops 2434793472 | bytes 21633024 | tf_op jit(solution)/shard_map/dot_general | solution.py:201
  206.2 40.6 %all-gather.11.cloned.1.call-done = bf16[1536,384]{1,0:T(8,128)(2,1)} async-done(((bf16[96,384]{1,0:T(8,128)(2,1)}), bf16[1536,384]{1,0:T(8,128)(2,1)}) %all-gather.11.cloned.1.call-update) | async-done | bytes 1179664 | tf_op jit(solution)/shard_map/all_gather | solution.py:196
  246.7 7.7 convolution_convert_fusion.2
  257.0 6.1 all_to_all.64
  267.5 2.7 fusion.125
  276.1 6.3 all_to_all.65
  282.4 12.4 %convert_reduce_fusion = (f32[1536]{0:T(1024)}, bf16[2048,1536]{1,0:T(8,128)(2,1)S(1)}) fusion(bf16[2048,384]{1,0:T(8,128)(2,1)S(1)} %bitcast.530, bf16[1536,384]{1,0:T(8,128)(2,1)S(1)} %copy-done.97, f32[2048,1536]{1,0:T(8,128)} %get-tuple-element.208, f32[1536]{0:T(1024)S(1)} %copy-done.92), kind=kOutput, calls=%fused_computation.5 | convolution fusion | flops 2466249216 | bytes 21639168 | tf_op jit(solution)/shard_map/dot_general | solution.py:213
  294.8 4.5 convolution_convert_fusion.1
  301.8 6.6 all_to_all.66
  320.0 23.8 %multiply_reduce_fusion.21 = (f32[2,512,6]{1,0,2:T(2,128)S(1)}, f32[2,512,6]{1,0,2:T(2,128)S(1)}, f32[2,512,6]{1,0,2:T(2,128)S(1)}, f32[2,512,6]{1,0,2:T(2,128)S...) fusion(f32[2,512,6,64]{1,0,3,2:T(2,128)} %reshape.468, ...), kind=kLoop, calls=%fused_computation.102 | loop fusion | flops 10561536 | bytes 17743872 | tf_op jit(solution)/shard_map/transpose(jvp())/reduce_sum | solution.py:70
  345.9 5.2 fusion.40
  351.4 8.2 fusion.131
  364.1 6.5 fusion
  370.6 6.8 fusion.2
  382.8 3.0 copy.161
  385.8 6.1 fusion.30
  391.9 7.7 fusion.27
  399.6 4.9 fusion.132
  404.6 3.1 fusion.19
  409.7 2.8 copy.174
  414.6 4.3 multiply_reduce_fusion.5
  418.9 6.3 pad_add_fusion.8
  425.3 10.4 %fusion.20 = bf16[2,512,6,64]{1,0,3,2:T(2,128)(2,1)S(1)} fusion(f32[2,512,6,64]{1,0,3,2:T(2,128)S(1)} %copy-done.23, f32[2,512,6,64]{1,0,3,2:T(2,128)S(1)} %copy-done.24, f32[2,512,6,64]{1,0,3,2:T(2,128)S(1)} %copy-done.25, f32[2,512,6,64]{1,0,3,2:T(2,128)S(1)} %copy-done.26, f32[2,512,6,64]{1,0,3,2:T(2,128)S(1)} %copy-done.27, ...), kind=kLoop, calls=%fused_computation.86 | loop fusion | flops 2752512 | bytes 11796480 | tf_op jit(solution)/shard_map/transpose(jvp())/convert_element_type | solution.py:26
  439.0 2.7 add_add_fusion.2
  441.8 5.8 copy.162
  447.6 5.7 reshape.455
  459.4 2.9 pad_add_fusion
  462.3 8.6 copy.164
  471.7 60.5 %multiply_reduce_fusion.9 = (f32[768]{0:T(1024)S(1)}, f32[768]{0:T(1024)S(1)}, f32[768]{0:T(1024)S(1)}, f32[768]{0:T(1024)S(1)}, f32[768]{0:T(1024)S(1)}, /*inde...) fusion(f32[2,512,768]{1,0,2:T(2,128)} %reshape.455, ...), kind=kLoop, calls=%fused_computation.49 | loop fusion | flops 19654656 | bytes 34655232 | tf_op jit(solution)/shard_map/transpose(jvp())/reduce_sum | solution.py:59
  532.4 39.5 %all-reduce.49 = (f32[9,768]{1,0:T(8,128)S(1)}, f32[4,768]{1,0:T(4,128)S(1)}) all-reduce(f32[9,768]{1,0:T(8,128)S(1)} %pad_add_fusion.16, f32[4,768]{1,0:T(4,128)S(1)} %add_add_fusion.3), channel_id=1, replica_groups=mesh['grp'=2,'dp'=16] {'grp','dp'}, use_global_device_ids=true, to_apply=%region_36.37 | all-reduce | flops 9984 | bytes 79872 | tf_op jit(solution)/shard_map/psum | solution.py:270
  573.3 14.2 %pad_add_fusion.1 = f32[2,520,768]{1,0,2:T(2,128)S(1)} fusion(f32[2,512,768]{1,0,2:T(2,128)} %get-tuple-element.146, f32[2,512,768]{1,0,2:T(2,128)} %get-tuple-element.147, f32[2,512,768]{1,0,2:T(2,128)} %get-tuple-element.148), kind=kLoop, calls=%fused_computation.25 | loop fusion | flops 1597440 | bytes 12632064 | tf_op jit(solution)/shard_map/transpose(jvp())/add_any | solution.py:59
  587.6 21.5 %fusion.13 = f32[2,512,768]{1,0,2:T(2,128)S(1)} fusion(f32[2,512,768]{1,0,2:T(2,128)} %copy.162, f32[2,512,768]{1,0,2:T(2,128)S(1)} %copy-done.7, f32[2,512,768]{1,0,2:T(2,128)S(1)} %copy-done.8, f32[2,512,768]{1,0,2:T(2,128)S(1)} %copy-done.9, f32[2,512,768]{1,0,2:T(2,128)S(1)} %copy-done.10, f32[2,512,768]{1,0,2:T(2,128)} %get-tuple-element.144, ...), kind=kLoop, calls=%fused_computation.32 | loop fusion | flops 5505024 | bytes 28311552 | tf_op jit(solution)/shard_map/transpose(jvp())/add_any | solution.py:52
  613.5 41.2 %all-reduce.48 = f32[1536]{0:T(1024)S(1)} all-reduce(f32[1536]{0:T(1024)S(1)} %copy-done.93), channel_id=5, replica_groups=mesh['grp'=2,'dp'=16] {'dp'}, use_global_device_ids=true, to_apply=%region_45.46.clone | all-reduce | flops 1536 | bytes 12288
  660.4 43.6 %reduce-scatter.9.cloned.1.call-done = f32[384,96]{0,1:T(8,128)} async-done(((f32[384,1536]{0,1:T(8,128)}), f32[384,96]{0,1:T(8,128)}) %reduce-scatter.9.cloned.1.call-update) | async-done | bytes 147472 | tf_op jit(solution)/shard_map/reduce_scatter | solution.py:266
  705.9 130.6 %reduce-scatter.11.cloned.1.call-done = f32[96,384]{1,0:T(8,128)} async-done(((f32[1536,384]{1,0:T(8,128)}), f32[96,384]{1,0:T(8,128)}) %reduce-scatter.11.cloned.1.call-update) | async-done | bytes 147472 | tf_op jit(solution)/shard_map/reduce_scatter | solution.py:268
  838.4 139.6 %reduce-scatter.5.cloned.1.call-done = f32[5,24,384]{2,0,1:T(8,128)} async-done(((f32[5,768,384]{2,0,1:T(8,128)}), f32[5,24,384]{2,0,1:T(8,128)}) %reduce-scatter.5.cloned.1.call-update) | async-done | bytes 184336 | tf_op jit(solution)/shard_map/reduce_scatter | solution.py:262
  (358 shorter events, 124.7 us)
Async XLA Ops:
  7.2 62.1 %copy-start.42 = (bf16[1024,768]{1,0:T(8,128)(2,1)S(1)}, bf16[1024,768]{1,0:T(8,128)(2,1)}, u32[]{:S(2)}) copy-start(bf16[1024,768]{1,0:T(8,128)(2,1)} %param.12) | copy-start | bytes 4718596
  7.2 108.7 %all-gather.5.cloned.1.call-start = ((), (), s32[]{:S(2)}) async-start(), calls=%async_computation.8 | async-start | bytes 3041280 | tf_op jit(solution)/shard_map/all_gather | solution.py:189
  9.0 170.4 %all-gather.7.cloned.1.call-start = ((), (), s32[]{:S(2)}) async-start(), calls=%async_computation.9 | async-start | bytes 1216512 | tf_op jit(solution)/shard_map/all_gather | solution.py:190
  10.5 183.3 %all-gather.9.cloned.1.call-start = ((), (), s32[]{:S(2)}) async-start(), calls=%async_computation.10 | async-start | bytes 1253376 | tf_op jit(solution)/shard_map/all_gather | solution.py:194
  12.2 234.6 %all-gather.11.cloned.1.call-start = ((), (), s32[]{:S(2)}) async-start(), calls=%async_computation.11 | async-start | bytes 1253376 | tf_op jit(solution)/shard_map/all_gather | solution.py:196
  65.0 10.0 %copy-start.77 = (f32[768]{0:T(1024)}, f32[768]{0:T(1024)S(1)}, u32[]{:S(2)}) copy-start(f32[768]{0:T(1024)S(1)} %get-tuple-element.105) | copy-start | bytes 9220
  118.4 27.4 %copy-start.4 = (bf16[1024,384]{1,0:T(8,128)(2,1)}, bf16[1024,384]{1,0:T(8,128)(2,1)S(1)}, u32[]{:S(2)}) copy-start(bf16[1024,384]{1,0:T(8,128)(2,1)S(1)} %convolution_convert_fusion.9) | copy-start | bytes 2359300
  132.7 38.2 %copy-start.29 = (bf16[2,512,6,64]{1,0,3,2:T(2,128)(2,1)}, bf16[2,512,6,64]{1,0,3,2:T(2,128)(2,1)S(1)}, u32[]{:S(2)}) copy-start(bf16[2,512,6,64]{1,0,3,2:T(2,128)(2,1)S(1)} %convert_element_type.275) | copy-start | bytes 2359300
  147.2 18.9 %copy-start.30 = (bf16[2,512,6,64]{1,0,3,2:T(2,128)(2,1)S(1)}, bf16[2,512,6,64]{1,0,3,2:T(2,128)(2,1)}, u32[]{:S(2)}) copy-start(bf16[2,512,6,64]{1,0,3,2:T(2,128)(2,1)} %convert_element_type.279) | copy-start | bytes 2359300
  147.2 18.9 %copy-start.98 = (s32[2]{0:T(128)S(1)}, s32[2]{0:T(128)}, u32[]{:S(2)}) copy-start(s32[2]{0:T(128)} %param.13) | copy-start | bytes 28
  147.3 18.7 %copy-start.40 = (bf16[2,512,6,64]{1,0,3,2:T(2,128)(2,1)S(1)}, bf16[2,512,6,64]{1,0,3,2:T(2,128)(2,1)}, u32[]{:S(2)}) copy-start(bf16[2,512,6,64]{1,0,3,2:T(2,128)(2,1)} %convert_element_type.277) | copy-start | bytes 2359300
  147.8 21.3 %copy-start.54 = (f32[2,512,6]{1,0,2:T(2,128)}, f32[2,512,6]{1,0,2:T(2,128)S(1)}, u32[]{:S(2)}) copy-start(f32[2,512,6]{1,0,2:T(2,128)S(1)} %get-tuple-element.186) | copy-start | bytes 73732
  147.8 21.3 %copy-start.55 = (f32[2,512,6]{1,0,2:T(2,128)}, f32[2,512,6]{1,0,2:T(2,128)S(1)}, u32[]{:S(2)}) copy-start(f32[2,512,6]{1,0,2:T(2,128)S(1)} %get-tuple-element.187) | copy-start | bytes 73732
  147.8 21.3 %copy-start.56 = (f32[2,512,6]{1,0,2:T(2,128)}, f32[2,512,6]{1,0,2:T(2,128)S(1)}, u32[]{:S(2)}) copy-start(f32[2,512,6]{1,0,2:T(2,128)S(1)} %get-tuple-element.188) | copy-start | bytes 73732
  188.5 7.2 all-to-all-start
  193.1 462.9 %all-reduce.52.cloned.1.call-start = ((), (), s32[]{:S(2)}) async-start(), calls=%async_computation.14 | async-start | bytes 172032 | tf_op jit(solution)/shard_map/psum | solution.py:270
  282.4 12.4 %copy-start.43 = (bf16[1024,2,384]{2,0,1:T(8,128)(2,1)}, bf16[1024,2,384]{2,0,1:T(8,128)(2,1)S(1)}, u32[]{:S(2)}) copy-start(bf16[1024,2,384]{2,0,1:T(8,128)(2,1)S(1)} %all_to_all.65) | copy-start | bytes 4718596
  282.4 12.4 %copy-start.96 = (bf16[384,1536]{0,1:T(8,128)(2,1)S(1)}, bf16[384,1536]{0,1:T(8,128)(2,1)}, u32[]{:S(2)}) copy-start(bf16[384,1536]{0,1:T(8,128)(2,1)} %all-gather.9.cloned.1.call-done) | copy-start | bytes 3538948
  320.0 23.8 %copy-start.64 = (f32[2,512,6]{1,0,2:T(2,128)S(1)}, f32[2,512,6]{1,0,2:T(2,128)}, u32[]{:S(2)}) copy-start(f32[2,512,6]{1,0,2:T(2,128)} %multiply_divide_fusion) | copy-start | bytes 73732
  320.0 24.9 %copy-start.5 = (bf16[1024,384]{1,0:T(8,128)(2,1)S(1)}, bf16[1024,384]{1,0:T(8,128)(2,1)}, u32[]{:S(2)}) copy-start(bf16[1024,384]{1,0:T(8,128)(2,1)} %copy-done.4) | copy-start | bytes 2359300
  320.0 24.9 %copy-start.14 = (bf16[1024,384]{1,0:T(8,128)(2,1)S(1)}, bf16[1024,384]{1,0:T(8,128)(2,1)}, u32[]{:S(2)}) copy-start(bf16[1024,384]{1,0:T(8,128)(2,1)} %copy-done.13) | copy-start | bytes 2359300
  345.9 312.7 %reduce-scatter.7.cloned.1.call-start = ((), (), s32[]{:S(2)}) async-start(), calls=%async_computation.13 | async-start | bytes 2433024 | tf_op jit(solution)/shard_map/reduce_scatter | solution.py:263
  351.1 352.8 %reduce-scatter.9.cloned.1.call-start = ((), (), s32[]{:S(2)}) async-start(), calls=%async_computation.15 | async-start | bytes 2506752 | tf_op jit(solution)/shard_map/reduce_scatter | solution.py:266
  359.7 476.8 %reduce-scatter.11.cloned.1.call-start = ((), (), s32[]{:S(2)}) async-start(), calls=%async_computation.16 | async-start | bytes 2506752 | tf_op jit(solution)/shard_map/reduce_scatter | solution.py:268
  385.8 13.7 %slice-start = ((s8[6291456]{0:T(1024)(128)(4,1)}), s8[4194304]{0:T(1024)(128)(4,1)S(1)}, s32[]{:S(2)}) async-start(s8[6291456]{0:T(1024)(128)(4,1)} %bitcast.557), calls=%async_computation.17 | async-start | bytes 8388608
  404.5 573.5 %reduce-scatter.5.cloned.1.call-start = ((), (), s32[]{:S(2)}) async-start(), calls=%async_computation.12 | async-start | bytes 9732096 | tf_op jit(solution)/shard_map/reduce_scatter | solution.py:262
  414.4 10.8 %copy-start.28 = (f32[2,512,6,64]{1,0,3,2:T(2,128)S(1)}, f32[2,512,6,64]{1,0,3,2:T(2,128)}, u32[]{:S(2)}) copy-start(f32[2,512,6,64]{1,0,3,2:T(2,128)} %get-tuple-element.155) | copy-start | bytes 4718596
  414.6 22.3 %copy-start.36 = (bf16[48,8,2,512]{3,1,2,0:T(8,128)(2,1)}, bf16[48,8,2,512]{3,1,2,0:T(8,128)(2,1)S(1)}, u32[]{:S(2)}) copy-start(bf16[48,8,2,512]{3,1,2,0:T(8,128)(2,1)S(1)} %copy.200) | copy-start | bytes 2359300
  414.6 10.6 %copy-start.27 = (f32[2,512,6,64]{1,0,3,2:T(2,128)S(1)}, f32[2,512,6,64]{1,0,3,2:T(2,128)}, u32[]{:S(2)}) copy-start(f32[2,512,6,64]{1,0,3,2:T(2,128)} %get-tuple-element.154) | copy-start | bytes 4718596
  425.3 10.6 %copy-start.34 = (bf16[48,8,2,512]{3,1,2,0:T(8,128)(2,1)S(1)}, bf16[48,8,2,512]{3,1,2,0:T(8,128)(2,1)}, u32[]{:S(2)}) copy-start(bf16[48,8,2,512]{3,1,2,0:T(8,128)(2,1)} %copy.199) | copy-start | bytes 2359300
  425.3 10.6 %copy-start.41 = (bf16[5,768,384]{2,1,0:T(8,128)(2,1)S(1)}, bf16[5,768,384]{2,1,0:T(8,128)(2,1)}, u32[]{:S(2)}) copy-start(bf16[5,768,384]{2,1,0:T(8,128)(2,1)} %all-gather.5.cloned.1.call-done) | copy-start | bytes 8847364
  471.7 100.2 %copy-start.53 = (f32[1,9,768]{2,0,1:T(1,128)S(1)}, f32[1,9,768]{2,0,1:T(1,128)}, u32[]{:S(2)}) copy-start(f32[1,9,768]{2,0,1:T(1,128)} %copy-done.52) | copy-start | bytes 82948
  471.7 100.2 %copy-start.61 = (f32[1,9,768]{2,0,1:T(1,128)S(1)}, f32[1,9,768]{2,0,1:T(1,128)}, u32[]{:S(2)}) copy-start(f32[1,9,768]{2,0,1:T(1,128)} %get-tuple-element.191) | copy-start | bytes 82948
  471.7 100.2 %copy-start.62 = (f32[1,9,768]{2,0,1:T(1,128)S(1)}, f32[1,9,768]{2,0,1:T(1,128)}, u32[]{:S(2)}) copy-start(f32[1,9,768]{2,0,1:T(1,128)} %get-tuple-element.192) | copy-start | bytes 82948
  471.7 100.2 %copy-start.63 = (f32[1,9,768]{2,0,1:T(1,128)S(1)}, f32[1,9,768]{2,0,1:T(1,128)}, u32[]{:S(2)}) copy-start(f32[1,9,768]{2,0,1:T(1,128)} %get-tuple-element.194) | copy-start | bytes 82948
  573.3 14.3 %copy-start.7 = (f32[2,512,768]{1,0,2:T(2,128)S(1)}, f32[2,512,768]{1,0,2:T(2,128)}, u32[]{:S(2)}) copy-start(f32[2,512,768]{1,0,2:T(2,128)} %get-tuple-element.140) | copy-start | bytes 9437188
  573.3 14.3 %copy-start.8 = (f32[2,512,768]{1,0,2:T(2,128)S(1)}, f32[2,512,768]{1,0,2:T(2,128)}, u32[]{:S(2)}) copy-start(f32[2,512,768]{1,0,2:T(2,128)} %get-tuple-element.141) | copy-start | bytes 9437188
  573.3 14.3 %copy-start.9 = (f32[2,512,768]{1,0,2:T(2,128)S(1)}, f32[2,512,768]{1,0,2:T(2,128)}, u32[]{:S(2)}) copy-start(f32[2,512,768]{1,0,2:T(2,128)} %get-tuple-element.142) | copy-start | bytes 9437188
  573.3 14.3 %copy-start.10 = (f32[2,512,768]{1,0,2:T(2,128)S(1)}, f32[2,512,768]{1,0,2:T(2,128)}, u32[]{:S(2)}) copy-start(f32[2,512,768]{1,0,2:T(2,128)} %get-tuple-element.143) | copy-start | bytes 9437188
  611.8 42.9 %copy-start.94 = (f32[4,1,96]{2,1,0:T(1,128)S(1)}, f32[4,1,96]{2,1,0:T(1,128)}, u32[]{:S(2)}) copy-start(f32[4,1,96]{2,1,0:T(1,128)} %param.20) | copy-start | bytes 4612
  611.9 43.5 %copy-start.65 = (f32[4,4,768]{2,1,0:T(4,128)S(1)}, f32[4,4,768]{2,1,0:T(4,128)}, u32[]{:S(2)}) copy-start(f32[4,4,768]{2,1,0:T(4,128)} %param.18) | copy-start | bytes 147460
  611.9 44.2 %copy-start.49 = (f32[1,384,54]{1,0,2:T(1,128)S(1)}, f32[1,384,54]{1,0,2:T(1,128)}, u32[]{:S(2)}) copy-start(f32[1,384,54]{1,0,2:T(1,128)} %get-tuple-element.176) | copy-start | bytes 248836
  611.9 44.2 %copy-start.50 = (f32[1,384,54]{1,0,2:T(1,128)S(1)}, f32[1,384,54]{1,0,2:T(1,128)}, u32[]{:S(2)}) copy-start(f32[1,384,54]{1,0,2:T(1,128)} %get-tuple-element.177) | copy-start | bytes 248836
  611.9 44.2 %copy-start.51 = (f32[1,384,54]{1,0,2:T(1,128)S(1)}, f32[1,384,54]{1,0,2:T(1,128)}, u32[]{:S(2)}) copy-start(f32[1,384,54]{1,0,2:T(1,128)} %get-tuple-element.179) | copy-start | bytes 248836
  611.9 46.7 %copy-start.48 = (f32[4,24,768]{2,1,0:T(8,128)S(1)}, f32[4,24,768]{2,1,0:T(8,128)}, u32[]{:S(2)}) copy-start(f32[4,24,768]{2,1,0:T(8,128)} %param.15) | copy-start | bytes 884740
  611.9 92.0 %copy-start.46 = (f32[4,1,384,96]{2,3,1,0:T(8,128)S(1)}, f32[4,1,384,96]{2,3,1,0:T(8,128)}, u32[]{:S(2)}) copy-start(f32[4,1,384,96]{2,3,1,0:T(8,128)} %param.19) | copy-start | bytes 1769476
  613.5 223.0 %copy-start.47 = (f32[4,1,96,384]{3,2,1,0:T(8,128)S(1)}, f32[4,1,96,384]{3,2,1,0:T(8,128)}, u32[]{:S(2)}) copy-start(f32[4,1,96,384]{3,2,1,0:T(8,128)} %param.21) | copy-start | bytes 1769476
  658.6 319.4 %copy-start.45 = (f32[4,5,24,384]{3,2,1,0:T(8,128)S(1)}, f32[4,5,24,384]{3,2,1,0:T(8,128)}, u32[]{:S(2)}) copy-start(f32[4,5,24,384]{3,2,1,0:T(8,128)} %param.14) | copy-start | bytes 2211844
  (64 other events, 264.7 us)
Sparse Core Ops, SparseCore 0:
  11.5 61.9 all-gather.4
  77.0 52.9 all-gather.6
  133.4 55.0 all-gather.8
  191.7 54.9 all-gather.10
  346.0 118.3 all-reduce.51
  469.5 100.9 reduce-scatter.6
  576.3 127.6 reduce-scatter.8
  708.9 127.5 reduce-scatter.10
  843.4 134.5 reduce-scatter.4
where the time goes:
time: 998 us; the launch traced here: 987 us
  waiting for transfers between devices  356 us (36%)
  other arithmetic  235 us (24%)
  blocking collectives  143 us (14%)
  matrix products  120 us (12%)
  local copies, waits for them, and re-layouts  110 us (11%)
  between operations  17.2 us (2%)
    reduce_scatter x1, waiting for transfers between devices, on_device(): lax.psum_scatter(d_mix, ('grp', 'dp'), scatter_dimension=1, tiled=True)  140 us
    reduce_scatter x1, waiting for transfers between devices, on_device(): lax.psum_scatter(d_down, 'dp', scatter_dimension=0, tiled=True)  131 us
    unnamed x2, blocking collectives  84.9 us
    reduce_sum x1, other arithmetic, front_part(): spread = spread + depth[offset] * padded[:, offset:offset + length]  60.5 us
    convert_element_type x4, other arithmetic, rounded(): return value.astype(jnp.bfloat16).astype(jnp.float32)  49.7 us
    reduce_scatter x1, waiting for transfers between devices, on_device(): lax.psum_scatter(d_up, 'dp', scatter_dimension=1, tiled=True)  43.6 us
    all_gather x1, waiting for transfers between devices, on_device(): lax.all_gather(down_state[0, 0].astype(jnp.bfloat16), 'dp', axis=0, tiled...  40.6 us
    psum x1, blocking collectives, on_device(): lax.psum((d_depth, d_span, d_norms_one + d_norms_two), ('grp', 'dp'))  39.5 us
  transfers between devices with their start and end apart: 10, of which 5 were waited for; matrix products, arithmetic and copies ran while one was open for 38% of the time, Pallas kernels for 0%

commit v1 on v0

--- a/solution.py
+++ b/solution.py
@@ -20,6 +20,18 @@
 rate_up = 0.08
 rate_bias = 0.3
 rate_down = 0.04
+
+
+def collect(array, axis, dim):
+    ways, here = (lax.axis_size(axis), lax.axis_index(axis))
+    grown, reach = (array, 1)
+    while reach < ways:
+        theirs = lax.ppermute(grown, axis, [(d, d ^ reach) for d in range(ways)])
+        mine_first = jnp.concatenate([grown, theirs], axis=dim)
+        theirs_first = jnp.concatenate([theirs, grown], axis=dim)
+        grown = jnp.where(here & reach == 0, mine_first, theirs_first)
+        reach = 2 * reach
+    return grown
 
 
 def rounded(value):
@@ -193,7 +205,7 @@
     up_all, bias_all, down_all = (
         lax.all_gather(up_state[0, 0].astype(jnp.bfloat16), "dp", axis=1, tiled=True),
         lax.all_gather(bias_state[0, 0].astype(jnp.bfloat16), "dp", axis=0, tiled=True),
-        lax.all_gather(down_state[0, 0].astype(jnp.bfloat16), "dp", axis=0, tiled=True),
+        collect(down_state[0, 0].astype(jnp.bfloat16), "dp", 0),
     )
     group_in = lax.all_to_all(
         normed.astype(jnp.bfloat16), "grp", split_axis=1, concat_axis=0, tiled=True

time: 998 us -> 954 us (0.956)
  waiting for transfers between devices: 356 us -> 318 us
    all_gather x1 -> x0, waiting for transfers between devices: 40.6 us -> none  [on_device(): lax.all_gather(down_state[0, 0].astype(jnp.bfloat16), 'dp', axis=0, tiled...]
    unnamed x226 -> x228, local copies, waits for them, and re-layouts: 30.5 us -> 30.9 us
  transfers between devices with their start and end apart: 10 -> 13, of which waited for: 5 -> 5; matrix products, arithmetic and copies ran while one was open for 38% -> 39% of each run, Pallas kernels for 0% -> 0%
where the time goes in v1:
time: 954 us; the launch traced here: 949 us
  waiting for transfers between devices  318 us (33%)
  other arithmetic  232 us (24%)
  blocking collectives  141 us (15%)
  matrix products  120 us (13%)
  local copies, waits for them, and re-layouts  108 us (11%)
  between operations  17.3 us (2%)
  starting transfers between devices  11.6 us (1%)
    reduce_scatter x1, waiting for transfers between devices, on_device(): lax.psum_scatter(d_mix, ('grp', 'dp'), scatter_dimension=1, tiled=True)  140 us
    reduce_scatter x1, waiting for transfers between devices, on_device(): lax.psum_scatter(d_down, 'dp', scatter_dimension=0, tiled=True)  131 us
    unnamed x2, blocking collectives  81.1 us
    reduce_sum x1, other arithmetic, front_part(): spread = spread + depth[offset] * padded[:, offset:offset + length]  60.4 us
    convert_element_type x4, other arithmetic, rounded(): return value.astype(jnp.bfloat16).astype(jnp.float32)  49.9 us
    reduce_scatter x1, waiting for transfers between devices, on_device(): lax.psum_scatter(d_up, 'dp', scatter_dimension=1, tiled=True)  42 us
    psum x1, blocking collectives, on_device(): lax.psum((d_depth, d_span, d_norms_one + d_norms_two), ('grp', 'dp'))  40.8 us
    unnamed x228, local copies, waits for them, and re-layouts  30.9 us
  transfers between devices with their start and end apart: 13, of which 5 were waited for; matrix products, arithmetic and copies ran while one was open for 39% of the time, Pallas kernels for 0%

profile of v1, /device:TPU:0, one launch (start us, length us, event | category | flops | bytes accessed | tf_op | source)
XLA Modules:
  0.0 948.5 jit_solution(3330183775668601924)
XLA Ops:
  11.4 3.0 collective-permute-start
  20.4 4.1 reshape.438
  24.6 39.1 %add_convert_fusion.3 = bf16[2,512,768]{1,0,2:T(2,128)(2,1)S(1)} fusion(f32[2,512,768]{1,0,2:T(2,128)} %reshape.438, f32[768]{0:T(1024)S(1)} %get-tuple-element.102, f32[768]{0:T(1024)S(1)} %get-tuple-element.103, f32[768]{0:T(1024)S(1)} %get-tuple-element.104, f32[768]{0:T(1024)S(1)} %get-tuple-element.105, f32[768]{0:T(1024)S(1)} %get-tuple-element.106, ...), kind=kLoop, calls=%fused_computation.58 | loop fusion | flops 14155776 | bytes 4746240 | tf_op jit(solution)/shard_map/jvp()/convert_element_type | solution.py:38
  66.0 3.1 collective-permute-done.1
  73.9 40.3 %all-reduce.47 = bf16[1536]{0:T(1024)(128)(2,1)S(1)} all-reduce(bf16[1536]{0:T(1024)(128)(2,1)S(1)} %dynamic-update-slice), channel_id=1, replica_groups=mesh['grp'=2,'dp'=16] {'dp'}, use_global_device_ids=true, to_apply=%add.47 | all-reduce | flops 1536 | bytes 6144
  126.3 3.4 convolution_convert_fusion.8
  138.8 3.9 fusion.22
  142.7 3.0 copy.141
  145.7 3.9 reshape.464
  154.2 4.0 fusion.132
  160.1 2.7 copy-done
  165.4 13.6 %add_convert_fusion.6 = bf16[2,512,6,64]{1,0,3,2:T(2,128)(2,1)S(1)} fusion(f32[2,512,6,64]{1,0,3,2:T(2,128)S(1)} %copy-done.6, f32[2,512,6]{1,0,2:T(2,128)S(1)} %get-tuple-element.181, f32[2,512,6]{1,0,2:T(2,128)S(1)} %get-tuple-element.182, f32[2,512,6]{1,0,2:T(2,128)S(1)} %get-tuple-element.183, f32[2,512,6]{1,0,2:T(2,128)S(1)} %get-tuple-element.184, ...), kind=kLoop, calls=%fused_computation.103 | loop fusion | flops 7077888 | bytes 2580480 | tf_op jit(solution)/shard_map/convert.9
  182.0 3.3 fusion.21
  191.1 4.6 all-to-all-start
  198.3 8.2 multiply_convert_fusion
  206.5 7.9 convolution_convert_fusion.2
  217.1 6.3 all_to_all.64
  236.3 6.3 all_to_all.65
  242.6 13.7 %convert_reduce_fusion = (f32[1536]{0:T(1024)}, bf16[2048,1536]{1,0:T(8,128)(2,1)S(1)}) fusion(bf16[2048,384]{1,0:T(8,128)(2,1)S(1)} %bitcast.528, bf16[768,384]{1,0:T(8,128)(2,1)} %collective-permute-done.3, bf16[768,384]{1,0:T(8,128)(2,1)} %maximum_select_fusion.1, pred[]{:T(512)S(6)} %eq.18, f32[2048,1536]{1,0:T(8,128)} %get-tuple-element.208, ...), kind=kOutput, calls=%fused_computation.5 | convolution fusion | flops 2471557632 | bytes 21639168 | tf_op jit(solution)/shard_map/dot_general | solution.py:225
  256.3 4.5 convolution_convert_fusion.1
  263.4 6.6 all_to_all.66
  281.6 23.8 %multiply_reduce_fusion.21 = (f32[2,512,6]{1,0,2:T(2,128)S(1)}, f32[2,512,6]{1,0,2:T(2,128)S(1)}, f32[2,512,6]{1,0,2:T(2,128)S(1)}, f32[2,512,6]{1,0,2:T(2,128)S...) fusion(f32[2,512,6,64]{1,0,3,2:T(2,128)} %reshape.468, ...), kind=kLoop, calls=%fused_computation.102 | loop fusion | flops 10561536 | bytes 17743872 | tf_op jit(solution)/shard_map/transpose(jvp())/reduce_sum | solution.py:82
  307.6 5.2 fusion.40
  313.3 8.2 fusion.133
  326.0 6.5 fusion
  332.5 6.6 fusion.2
  344.5 3.0 copy.161
  347.5 6.1 fusion.30
  353.6 7.7 fusion.27
  361.3 4.9 fusion.134
  366.3 3.1 fusion.19
  371.3 2.8 copy.174
  376.3 4.3 multiply_reduce_fusion.5
  380.6 6.3 pad_add_fusion.8
  387.0 10.6 %fusion.20 = bf16[2,512,6,64]{1,0,3,2:T(2,128)(2,1)S(1)} fusion(f32[2,512,6,64]{1,0,3,2:T(2,128)S(1)} %copy-done.24, f32[2,512,6,64]{1,0,3,2:T(2,128)S(1)} %copy-done.25, f32[2,512,6,64]{1,0,3,2:T(2,128)S(1)} %copy-done.26, f32[2,512,6,64]{1,0,3,2:T(2,128)S(1)} %copy-done.27, f32[2,512,6,64]{1,0,3,2:T(2,128)S(1)} %copy-done.28, ...), kind=kLoop, calls=%fused_computation.86 | loop fusion | flops 2752512 | bytes 11796480 | tf_op jit(solution)/shard_map/transpose(jvp())/convert_element_type | solution.py:38
  400.9 2.7 add_add_fusion.2
  403.7 5.8 copy.162
  409.4 5.7 reshape.455
  421.3 2.9 pad_add_fusion
  424.2 8.6 copy.164
  433.6 60.4 %multiply_reduce_fusion.9 = (f32[768]{0:T(1024)S(1)}, f32[768]{0:T(1024)S(1)}, f32[768]{0:T(1024)S(1)}, f32[768]{0:T(1024)S(1)}, f32[768]{0:T(1024)S(1)}, /*inde...) fusion(f32[2,512,768]{1,0,2:T(2,128)} %reshape.455, ...), kind=kLoop, calls=%fused_computation.49 | loop fusion | flops 19654656 | bytes 34655232 | tf_op jit(solution)/shard_map/transpose(jvp())/reduce_sum | solution.py:71
  494.2 40.8 %all-reduce.49 = (f32[9,768]{1,0:T(8,128)S(1)}, f32[4,768]{1,0:T(4,128)S(1)}) all-reduce(f32[9,768]{1,0:T(8,128)S(1)} %pad_add_fusion.16, f32[4,768]{1,0:T(4,128)S(1)} %add_add_fusion.3), channel_id=1, replica_groups=mesh['grp'=2,'dp'=16] {'grp','dp'}, use_global_device_ids=true, to_apply=%region_36.37 | all-reduce | flops 9984 | bytes 79872 | tf_op jit(solution)/shard_map/psum | solution.py:282
  536.5 14.2 %pad_add_fusion.1 = f32[2,520,768]{1,0,2:T(2,128)S(1)} fusion(f32[2,512,768]{1,0,2:T(2,128)} %get-tuple-element.146, f32[2,512,768]{1,0,2:T(2,128)} %get-tuple-element.147, f32[2,512,768]{1,0,2:T(2,128)} %get-tuple-element.148), kind=kLoop, calls=%fused_computation.25 | loop fusion | flops 1597440 | bytes 12632064 | tf_op jit(solution)/shard_map/transpose(jvp())/add_any | solution.py:71
  550.8 21.5 %fusion.13 = f32[2,512,768]{1,0,2:T(2,128)S(1)} fusion(f32[2,512,768]{1,0,2:T(2,128)} %copy.162, f32[2,512,768]{1,0,2:T(2,128)S(1)} %copy-done.8, f32[2,512,768]{1,0,2:T(2,128)S(1)} %copy-done.9, f32[2,512,768]{1,0,2:T(2,128)S(1)} %copy-done.10, f32[2,512,768]{1,0,2:T(2,128)S(1)} %copy-done.11, f32[2,512,768]{1,0,2:T(2,128)} %get-tuple-element.144, ...), kind=kLoop, calls=%fused_computation.32 | loop fusion | flops 5505024 | bytes 28311552 | tf_op jit(solution)/shard_map/transpose(jvp())/add_any | solution.py:64
  576.7 40.8 %all-reduce.48 = f32[1536]{0:T(1024)S(1)} all-reduce(f32[1536]{0:T(1024)S(1)} %copy-done.93), channel_id=5, replica_groups=mesh['grp'=2,'dp'=16] {'dp'}, use_global_device_ids=true, to_apply=%region_45.46.clone | all-reduce | flops 1536 | bytes 12288
  623.2 42.0 %reduce-scatter.9.cloned.1.call-done = f32[384,96]{0,1:T(8,128)} async-done(((f32[384,1536]{0,1:T(8,128)}), f32[384,96]{0,1:T(8,128)}) %reduce-scatter.9.cloned.1.call-update) | async-done | bytes 147472 | tf_op jit(solution)/shard_map/reduce_scatter | solution.py:278
  667.2 130.6 %reduce-scatter.11.cloned.1.call-done = f32[96,384]{1,0:T(8,128)} async-done(((f32[1536,384]{1,0:T(8,128)}), f32[96,384]{1,0:T(8,128)}) %reduce-scatter.11.cloned.1.call-update) | async-done | bytes 147472 | tf_op jit(solution)/shard_map/reduce_scatter | solution.py:280
  799.7 139.7 %reduce-scatter.5.cloned.1.call-done = f32[5,24,384]{2,0,1:T(8,128)} async-done(((f32[5,768,384]{2,0,1:T(8,128)}), f32[5,24,384]{2,0,1:T(8,128)}) %reduce-scatter.5.cloned.1.call-update) | async-done | bytes 184336 | tf_op jit(solution)/shard_map/reduce_scatter | solution.py:274
  (368 shorter events, 130.7 us)
Async XLA Ops:
  7.2 114.8 %all-gather.4.cloned.1.call-start = ((), (), s32[]{:S(2)}) async-start(), calls=%async_computation.8 | async-start | bytes 3041280 | tf_op jit(solution)/shard_map/all_gather | solution.py:201
  8.8 173.1 %all-gather.6.cloned.1.call-start = ((), (), s32[]{:S(2)}) async-start(), calls=%async_computation.9 | async-start | bytes 1216512 | tf_op jit(solution)/shard_map/all_gather | solution.py:202
  10.4 186.0 %all-gather.8.cloned.1.call-start = ((), (), s32[]{:S(2)}) async-start(), calls=%async_computation.10 | async-start | bytes 1253376 | tf_op jit(solution)/shard_map/all_gather | solution.py:206
  11.4 52.4 %collective-permute-start = (bf16[96,384]{1,0:T(8,128)(2,1)S(1)}, bf16[96,384]{1,0:T(8,128)(2,1)S(1)}, u32[]{:S(2)}, u32[]{:S(2)}) collective-permute-start(bf16[96,384]{1,0:T(8,128)(2,1)S(1)} %bitcast_convert_fusion.1), channel_id=1, source_target_pairs={{0,1},{1,0},{2,3},{3,2},{4,5},{5,4},{6,7},{7,6},{8,9},{9,8},{10,11... | collective-permute-start | bytes 221192 | tf_op jit(solution)/shard_map/ppermute | solution.py:29
  24.5 47.9 %copy-start.94 = (u32[32]{0:T(128)S(1)}, u32[32]{0:T(128)}, u32[]{:S(2)}) copy-start(u32[32]{0:T(128)} %constant.268) | copy-start | bytes 388
  63.8 5.4 collective-permute-start.1
  69.3 50.6 %collective-permute-start.2 = (bf16[384,384]{1,0:T(8,128)(2,1)S(1)}, bf16[384,384]{1,0:T(8,128)(2,1)}, u32[]{:S(2)}, u32[]{:S(2)}) collective-permute-start(bf16[384,384]{1,0:T(8,128)(2,1)S(1)} %maximum_select_fusion.2), channel_id=1, source_target_pairs={{0,4},{1,5},{2,6},{3,7},{4,0},{5,1},{6,2},{7,3},{8,12},{9,13},{10,... | collective-permute-start | bytes 884744 | tf_op jit(solution)/shard_map/ppermute | solution.py:29
  121.9 84.6 %collective-permute-start.3 = (bf16[768,384]{1,0:T(8,128)(2,1)}, bf16[768,384]{1,0:T(8,128)(2,1)}, u32[]{:S(2)}, u32[]{:S(2)}) collective-permute-start(bf16[768,384]{1,0:T(8,128)(2,1)} %maximum_select_fusion.1), channel_id=1, source_target_pairs={{0,8},{1,9},{2,10},{3,11},{4,12},{5,13},{6,14},{7,15},{8,0},{9,1},... | collective-permute-start | bytes 1769480 | tf_op jit(solution)/shard_map/ppermute | solution.py:29
  124.5 27.8 %copy-start.4 = (bf16[1024,384]{1,0:T(8,128)(2,1)}, bf16[1024,384]{1,0:T(8,128)(2,1)S(1)}, u32[]{:S(2)}) copy-start(bf16[1024,384]{1,0:T(8,128)(2,1)S(1)} %convolution_convert_fusion.9) | copy-start | bytes 2359300
  138.8 21.3 %copy-start.30 = (bf16[2,512,6,64]{1,0,3,2:T(2,128)(2,1)}, bf16[2,512,6,64]{1,0,3,2:T(2,128)(2,1)S(1)}, u32[]{:S(2)}) copy-start(bf16[2,512,6,64]{1,0,3,2:T(2,128)(2,1)S(1)} %convert_element_type.275) | copy-start | bytes 2359300
  154.1 11.2 %copy-start.53 = (f32[2,512,6]{1,0,2:T(2,128)}, f32[2,512,6]{1,0,2:T(2,128)S(1)}, u32[]{:S(2)}) copy-start(f32[2,512,6]{1,0,2:T(2,128)S(1)} %get-tuple-element.186) | copy-start | bytes 73732
  154.2 11.2 %copy-start.54 = (f32[2,512,6]{1,0,2:T(2,128)}, f32[2,512,6]{1,0,2:T(2,128)S(1)}, u32[]{:S(2)}) copy-start(f32[2,512,6]{1,0,2:T(2,128)S(1)} %get-tuple-element.187) | copy-start | bytes 73732
  154.2 11.2 %copy-start.55 = (f32[2,512,6]{1,0,2:T(2,128)}, f32[2,512,6]{1,0,2:T(2,128)S(1)}, u32[]{:S(2)}) copy-start(f32[2,512,6]{1,0,2:T(2,128)S(1)} %get-tuple-element.188) | copy-start | bytes 73732
  191.1 7.2 all-to-all-start
  195.7 423.2 %all-reduce.52.cloned.1.call-start = ((), (), s32[]{:S(2)}) async-start(), calls=%async_computation.13 | async-start | bytes 172032 | tf_op jit(solution)/shard_map/psum | solution.py:282
  242.6 13.7 %copy-start.41 = (bf16[1024,2,384]{2,0,1:T(8,128)(2,1)}, bf16[1024,2,384]{2,0,1:T(8,128)(2,1)S(1)}, u32[]{:S(2)}) copy-start(bf16[1024,2,384]{2,0,1:T(8,128)(2,1)S(1)} %all_to_all.65) | copy-start | bytes 4718596
  242.6 13.7 %copy-start.97 = (bf16[384,1536]{0,1:T(8,128)(2,1)S(1)}, bf16[384,1536]{0,1:T(8,128)(2,1)}, u32[]{:S(2)}) copy-start(bf16[384,1536]{0,1:T(8,128)(2,1)} %all-gather.8.cloned.1.call-done) | copy-start | bytes 3538948
  281.6 23.8 %copy-start.63 = (f32[2,512,6]{1,0,2:T(2,128)S(1)}, f32[2,512,6]{1,0,2:T(2,128)}, u32[]{:S(2)}) copy-start(f32[2,512,6]{1,0,2:T(2,128)} %multiply_divide_fusion) | copy-start | bytes 73732
  281.6 24.9 %copy-start.5 = (bf16[1024,384]{1,0:T(8,128)(2,1)S(1)}, bf16[1024,384]{1,0:T(8,128)(2,1)}, u32[]{:S(2)}) copy-start(bf16[1024,384]{1,0:T(8,128)(2,1)} %copy-done.4) | copy-start | bytes 2359300
  281.6 24.9 %copy-start.15 = (bf16[1024,384]{1,0:T(8,128)(2,1)S(1)}, bf16[1024,384]{1,0:T(8,128)(2,1)}, u32[]{:S(2)}) copy-start(bf16[1024,384]{1,0:T(8,128)(2,1)} %copy-done.14) | copy-start | bytes 2359300
  307.5 313.9 %reduce-scatter.7.cloned.1.call-start = ((), (), s32[]{:S(2)}) async-start(), calls=%async_computation.12 | async-start | bytes 2433024 | tf_op jit(solution)/shard_map/reduce_scatter | solution.py:275
  312.8 9.5 copy-start.33
  312.8 352.5 %reduce-scatter.9.cloned.1.call-start = ((), (), s32[]{:S(2)}) async-start(), calls=%async_computation.14 | async-start | bytes 2506752 | tf_op jit(solution)/shard_map/reduce_scatter | solution.py:278
  321.5 476.2 %reduce-scatter.11.cloned.1.call-start = ((), (), s32[]{:S(2)}) async-start(), calls=%async_computation.15 | async-start | bytes 2506752 | tf_op jit(solution)/shard_map/reduce_scatter | solution.py:280
  347.5 13.8 %slice-start = ((s8[6291456]{0:T(1024)(128)(4,1)}), s8[4194304]{0:T(1024)(128)(4,1)S(1)}, s32[]{:S(2)}) async-start(s8[6291456]{0:T(1024)(128)(4,1)} %bitcast.555), calls=%async_computation.16 | async-start | bytes 8388608
  366.2 573.2 %reduce-scatter.5.cloned.1.call-start = ((), (), s32[]{:S(2)}) async-start(), calls=%async_computation.11 | async-start | bytes 9732096 | tf_op jit(solution)/shard_map/reduce_scatter | solution.py:274
  376.1 10.8 %copy-start.29 = (f32[2,512,6,64]{1,0,3,2:T(2,128)S(1)}, f32[2,512,6,64]{1,0,3,2:T(2,128)}, u32[]{:S(2)}) copy-start(f32[2,512,6,64]{1,0,3,2:T(2,128)} %get-tuple-element.155) | copy-start | bytes 4718596
  376.2 22.5 %copy-start.36 = (bf16[48,8,2,512]{3,1,2,0:T(8,128)(2,1)}, bf16[48,8,2,512]{3,1,2,0:T(8,128)(2,1)S(1)}, u32[]{:S(2)}) copy-start(bf16[48,8,2,512]{3,1,2,0:T(8,128)(2,1)S(1)} %copy.200) | copy-start | bytes 2359300
  376.3 10.6 %copy-start.28 = (f32[2,512,6,64]{1,0,3,2:T(2,128)S(1)}, f32[2,512,6,64]{1,0,3,2:T(2,128)}, u32[]{:S(2)}) copy-start(f32[2,512,6,64]{1,0,3,2:T(2,128)} %get-tuple-element.154) | copy-start | bytes 4718596
  387.0 10.8 %copy-start.34 = (bf16[48,8,2,512]{3,1,2,0:T(8,128)(2,1)S(1)}, bf16[48,8,2,512]{3,1,2,0:T(8,128)(2,1)}, u32[]{:S(2)}) copy-start(bf16[48,8,2,512]{3,1,2,0:T(8,128)(2,1)} %copy.199) | copy-start | bytes 2359300
  387.0 10.8 %copy-start.40 = (bf16[5,768,384]{2,1,0:T(8,128)(2,1)S(1)}, bf16[5,768,384]{2,1,0:T(8,128)(2,1)}, u32[]{:S(2)}) copy-start(bf16[5,768,384]{2,1,0:T(8,128)(2,1)} %all-gather.4.cloned.1.call-done) | copy-start | bytes 8847364
  433.6 101.5 %copy-start.52 = (f32[1,9,768]{2,0,1:T(1,128)S(1)}, f32[1,9,768]{2,0,1:T(1,128)}, u32[]{:S(2)}) copy-start(f32[1,9,768]{2,0,1:T(1,128)} %copy-done.51) | copy-start | bytes 82948
  433.6 101.5 %copy-start.60 = (f32[1,9,768]{2,0,1:T(1,128)S(1)}, f32[1,9,768]{2,0,1:T(1,128)}, u32[]{:S(2)}) copy-start(f32[1,9,768]{2,0,1:T(1,128)} %get-tuple-element.191) | copy-start | bytes 82948
  433.6 101.5 %copy-start.61 = (f32[1,9,768]{2,0,1:T(1,128)S(1)}, f32[1,9,768]{2,0,1:T(1,128)}, u32[]{:S(2)}) copy-start(f32[1,9,768]{2,0,1:T(1,128)} %get-tuple-element.192) | copy-start | bytes 82948
  433.6 101.5 %copy-start.62 = (f32[1,9,768]{2,0,1:T(1,128)S(1)}, f32[1,9,768]{2,0,1:T(1,128)}, u32[]{:S(2)}) copy-start(f32[1,9,768]{2,0,1:T(1,128)} %get-tuple-element.194) | copy-start | bytes 82948
  536.5 14.3 %copy-start.8 = (f32[2,512,768]{1,0,2:T(2,128)S(1)}, f32[2,512,768]{1,0,2:T(2,128)}, u32[]{:S(2)}) copy-start(f32[2,512,768]{1,0,2:T(2,128)} %get-tuple-element.140) | copy-start | bytes 9437188
  536.5 14.3 %copy-start.9 = (f32[2,512,768]{1,0,2:T(2,128)S(1)}, f32[2,512,768]{1,0,2:T(2,128)}, u32[]{:S(2)}) copy-start(f32[2,512,768]{1,0,2:T(2,128)} %get-tuple-element.141) | copy-start | bytes 9437188
  536.5 14.3 %copy-start.10 = (f32[2,512,768]{1,0,2:T(2,128)S(1)}, f32[2,512,768]{1,0,2:T(2,128)}, u32[]{:S(2)}) copy-start(f32[2,512,768]{1,0,2:T(2,128)} %get-tuple-element.142) | copy-start | bytes 9437188
  536.5 14.3 %copy-start.11 = (f32[2,512,768]{1,0,2:T(2,128)S(1)}, f32[2,512,768]{1,0,2:T(2,128)}, u32[]{:S(2)}) copy-start(f32[2,512,768]{1,0,2:T(2,128)} %get-tuple-element.143) | copy-start | bytes 9437188
  575.0 42.5 %copy-start.95 = (f32[4,1,96]{2,1,0:T(1,128)S(1)}, f32[4,1,96]{2,1,0:T(1,128)}, u32[]{:S(2)}) copy-start(f32[4,1,96]{2,1,0:T(1,128)} %param.20) | copy-start | bytes 4612
  575.1 43.2 %copy-start.64 = (f32[4,4,768]{2,1,0:T(4,128)S(1)}, f32[4,4,768]{2,1,0:T(4,128)}, u32[]{:S(2)}) copy-start(f32[4,4,768]{2,1,0:T(4,128)} %param.18) | copy-start | bytes 147460
  575.1 43.8 %copy-start.48 = (f32[1,384,54]{1,0,2:T(1,128)S(1)}, f32[1,384,54]{1,0,2:T(1,128)}, u32[]{:S(2)}) copy-start(f32[1,384,54]{1,0,2:T(1,128)} %get-tuple-element.176) | copy-start | bytes 248836
  575.1 43.8 %copy-start.49 = (f32[1,384,54]{1,0,2:T(1,128)S(1)}, f32[1,384,54]{1,0,2:T(1,128)}, u32[]{:S(2)}) copy-start(f32[1,384,54]{1,0,2:T(1,128)} %get-tuple-element.177) | copy-start | bytes 248836
  575.1 43.8 %copy-start.50 = (f32[1,384,54]{1,0,2:T(1,128)S(1)}, f32[1,384,54]{1,0,2:T(1,128)}, u32[]{:S(2)}) copy-start(f32[1,384,54]{1,0,2:T(1,128)} %get-tuple-element.179) | copy-start | bytes 248836
  575.1 46.3 %copy-start.46 = (f32[4,24,768]{2,1,0:T(8,128)S(1)}, f32[4,24,768]{2,1,0:T(8,128)}, u32[]{:S(2)}) copy-start(f32[4,24,768]{2,1,0:T(8,128)} %param.15) | copy-start | bytes 884740
  575.1 90.1 %copy-start.44 = (f32[4,1,384,96]{2,3,1,0:T(8,128)S(1)}, f32[4,1,384,96]{2,3,1,0:T(8,128)}, u32[]{:S(2)}) copy-start(f32[4,1,384,96]{2,3,1,0:T(8,128)} %param.19) | copy-start | bytes 1769476
  576.7 221.1 %copy-start.45 = (f32[4,1,96,384]{3,2,1,0:T(8,128)S(1)}, f32[4,1,96,384]{3,2,1,0:T(8,128)}, u32[]{:S(2)}) copy-start(f32[4,1,96,384]{3,2,1,0:T(8,128)} %param.21) | copy-start | bytes 1769476
  621.4 318.0 %copy-start.43 = (f32[4,5,24,384]{3,2,1,0:T(8,128)S(1)}, f32[4,5,24,384]{3,2,1,0:T(8,128)}, u32[]{:S(2)}) copy-start(f32[4,5,24,384]{3,2,1,0:T(8,128)} %param.14) | copy-start | bytes 2211844
  (68 other events, 239.4 us)
Sparse Core Ops, SparseCore 0:
  11.5 61.9 all-gather.3
  76.9 56.4 all-gather.5
  136.8 57.3 all-gather.7
  307.6 118.1 all-reduce.51
  431.0 101.0 reduce-scatter.6
  537.6 127.5 reduce-scatter.8
  670.2 127.5 reduce-scatter.10
  804.7 134.7 reduce-scatter.4
